TPU v7x, 32 devices: a whole 2x2x4 slice. The times are simulated.
32 devices in a mesh: rep: 2 (over y), fsdp: 4 (over z), section: 4 (over x, core).
Axes of the slice: x: 2, y: 2, z: 4, core: 2. Of those that a mesh axis runs over, the one named last changes fastest.
Arguments:
- iterate: bfloat16 [8, 3072, 1024], P(('rep', 'section'), None, 'fsdp'), parts along dimension 0, may hold values from -0.1875 to 0.1875
Outputs:
- update: bfloat16 [8, 3072, 1024], P(('rep', 'section'), None, 'fsdp'), parts along dimension 0
There are 2 independent parts, one for each index of `rep`. A program takes and returns all parts, laid end to end along the dimension named above; each array names one. Nothing has to cross between parts.
All inputs are finite; a program needn't handle non-finite values.
Results may differ from a plain program's by a relative error of at most 0.0055.
Values may be sent and summed in bfloat16 or wider, within the bound.
A program may use at most 128 MiB of HBM per device.

v0:
```python
import math
import jax
import jax.numpy as jnp
import numpy as np
from jax import lax
from jax.sharding import PartitionSpec as P


def tile_table(devices, band_blocks):
    block_table = np.zeros((devices, devices), dtype=np.int32)
    for row_block in range(devices):
        for col_block in range(devices):
            distance = (col_block - row_block) % devices
            if distance <= devices // 2:
                block_table[row_block, col_block] = row_block * band_blocks + distance
            else:
                block_table[row_block, col_block] = (
                    devices * band_blocks + col_block * band_blocks + (devices - distance)
                )
    return block_table


def on_device(iterate):
    devices = lax.axis_size("fsdp")
    experts, rows_all, columns = iterate.shape
    strip_rows = rows_all // devices
    band_blocks = devices // 2 + 1
    out_scale = 0.2 * math.sqrt(max(rows_all, columns * devices))
    expert_rows = iterate[0]
    row_blocks = expert_rows.reshape(devices, strip_rows, columns)

    def one_offset(offset):
        partner = jnp.roll(row_blocks, -offset, axis=0)
        tiles = jnp.einsum("nsc,ntc->nst", row_blocks, partner, preferred_element_type=jnp.float32)
        return tiles.astype(jnp.bfloat16)

    band_term = lax.map(one_offset, jnp.arange(band_blocks, dtype=jnp.int32))
    received = lax.all_to_all(band_term, "fsdp", split_axis=1, concat_axis=1, tiled=True)
    own_band = jnp.sum(received.astype(jnp.float32), axis=1).astype(jnp.bfloat16)
    upper_tiles = lax.all_gather(own_band, "fsdp", axis=0, tiled=True)
    tile_pool = jnp.concatenate([upper_tiles, jnp.swapaxes(upper_tiles, 1, 2)], axis=0)
    block_table = jnp.asarray(tile_table(devices, band_blocks))
    dense_blocks = jnp.take(tile_pool, block_table, axis=0)

    def apply_gram(operand):
        shaped = operand.reshape(devices, strip_rows, columns)
        product = jnp.einsum(
            "nmij,mjc->nic", dense_blocks, shaped, preferred_element_type=jnp.float32
        )
        return product.reshape(rows_all, columns)

    first_product = apply_gram(expert_rows)
    second_product = apply_gram(first_product.astype(jnp.bfloat16))
    combined = out_scale * (
        3.4445 * expert_rows.astype(jnp.float32) - 4.775 * first_product + 2.0315 * second_product
    )
    results = [combined.astype(jnp.bfloat16)]
    return jnp.stack(results)


def on_device_columns(iterate):
    devices = lax.axis_size("fsdp")
    own = lax.axis_index("fsdp")
    _, rows_all, columns = iterate.shape
    out_scale = 0.2 * math.sqrt(max(rows_all, columns * devices))
    gathered = lax.all_gather(iterate[0], "fsdp", axis=1, tiled=True)
    gram = lax.dot_general(
        gathered, gathered, (((0,), (0,)), ((), ())), preferred_element_type=jnp.float32
    )
    gram_half = gram.astype(jnp.bfloat16)
    own_gram = lax.dynamic_slice_in_dim(gram, own * columns, columns, 1)
    square = jnp.dot(gram_half, own_gram.astype(jnp.bfloat16), preferred_element_type=jnp.float32)
    row_ids = lax.broadcasted_iota(jnp.int32, square.shape, 0)
    column_ids = lax.broadcasted_iota(jnp.int32, square.shape, 1) + own * columns
    identity = (row_ids == column_ids).astype(jnp.float32)
    mixing = out_scale * (3.4445 * identity - 4.775 * own_gram + 2.0315 * square)
    update = jnp.dot(gathered, mixing.astype(jnp.bfloat16), preferred_element_type=jnp.float32)
    return update.astype(jnp.bfloat16)[None]


def for_shapes(iterate):
    _, rows_all, columns = iterate.shape
    if columns * lax.axis_size("fsdp") <= rows_all:
        return on_device_columns(iterate)
    return on_device(iterate)


def solution(mesh):
    return jax.shard_map(
        for_shapes,
        mesh=mesh,
        in_specs=(P(("rep", "section"), None, "fsdp"),),
        out_specs=P(("rep", "section"), None, "fsdp"),
        check_vma=False,
    )
```

profile of v0, /device:TPU:0, one launch (start us, length us, event | category | flops | bytes accessed | tf_op | source)
XLA Modules:
  0.0 155.0 jit_solution(9944123637097311542)
XLA Ops:
  6.5 0.0 all-gather.3.cloned.1.call-start
  6.5 0.7 all-gather.3.cloned.1.call-update
  7.3 119.2 %all-gather.3.cloned.1.call-done = bf16[1,3072,1024]{2,1,0:T(8,128)(2,1)} async-done(((bf16[1,3072,256]{2,1,0:T(8,128)(2,1)}), bf16[1,3072,1024]{2,1,0:T(8,128)(2,1)}) %all-gather.3.cloned.1.call-update) | async-done | bytes 6291472 | tf_op jit(solution)/shard_map/all_gather | solution.py:66
  126.5 12.0 %fusion.2 = f32[1024,1024]{1,0:T(8,128)} fusion(bf16[1,3072,1024]{2,1,0:T(8,128)(2,1)} %all-gather.3.cloned.1.call-done), kind=kOutput, calls=%fused_computation.2 | convolution fusion | flops 6442450944 | bytes 10485760 | tf_op jit(solution)/shard_map/dot_general | solution.py:67
  138.5 8.1 %fusion.7 = bf16[1,3072,256]{1,2,0:T(8,128)(2,1)S(1)} fusion(bf16[1,3072,1024]{2,1,0:T(8,128)(2,1)} %all-gather.3.cloned.1.call-done, f32[1024,1024]{1,0:T(8,128)} %fusion.2, s32[]{:T(128)S(6)} %select_n.3, s32[256]{0:T(256)S(1)} %iota_add_fusion), kind=kOutput, calls=%fused_computation.5 | convolution fusion | flops 2151677952 | bytes 14157824 | tf_op jit(solution)/shard_map/dot_general | solution.py:77
  146.6 1.6 %copy.2 = bf16[1,3072,256]{2,1,0:T(8,128)(2,1)} copy(bf16[1,3072,256]{1,2,0:T(8,128)(2,1)S(1)} %fusion.7) | data formatting | bytes 3145728 | tf_op jit(solution)/shard_map/broadcast_in_dim | solution.py:78
  (1 shorter events, 0.0 us)
Async XLA Ops:
  6.5 120.0 %all-gather.3.cloned.1.call-start = ((), (), s32[]{:S(2)}) async-start(), calls=%async_computation | async-start | bytes 7864320 | tf_op jit(solution)/shard_map/all_gather | solution.py:66
Sparse Core Ops, SparseCore 0:
  8.9 117.5 all-gather.2
where the time goes:
time: 155 us
  waiting for transfers between devices  120 us (77%)
  matrix products  20.1 us (13%)
  between operations  13.4 us (9%)
  local copies, waits for them, and re-layouts  1.57 us (1%)
    all_gather x1, waiting for transfers between devices, on_device_columns(): gathered = lax.all_gather(iterate[0], 'fsdp', axis=1, tiled=True)  119 us
    dot_general x1, matrix products, on_device_columns(): lax.dot_general(gathered, gathered, (((0,), (0,)), ((), ())), preferred_e...  12 us
    dot_general x1, matrix products, on_device_columns(): jnp.dot(gathered, mixing.astype(jnp.bfloat16), preferred_element_type=jnp...  8.06 us
  transfers between devices with their start and end apart: 1, of which 1 were waited for; matrix products, arithmetic and copies ran while one was open for 0% of the time, Pallas kernels for 0%

commit v1 on v0

--- a/solution.py
+++ b/solution.py
@@ -63,7 +63,26 @@
     own = lax.axis_index("fsdp")
     _, rows_all, columns = iterate.shape
     out_scale = 0.2 * math.sqrt(max(rows_all, columns * devices))
-    gathered = lax.all_gather(iterate[0], "fsdp", axis=1, tiled=True)
+    count, index, rows = (lax.axis_size("fsdp"), lax.axis_index("fsdp"), iterate[0].shape[1])
+    upward = [(i, (i + 1) % count) for i in range(count)]
+    backward = [(i, (i - 1) % count) for i in range(count)]
+    filled = jnp.zeros(
+        (*iterate[0].shape[:1], count * rows, *iterate[0].shape[1 + 1 :]), iterate[0].dtype
+    )
+    filled = lax.dynamic_update_slice_in_dim(filled, iterate[0], index * rows, axis=1)
+    from_left = from_right = iterate[0]
+    halfway = count // 2
+    for lap in range(1, halfway + 1):
+        from_left = lax.ppermute(from_left, "fsdp", upward)
+        filled = lax.dynamic_update_slice_in_dim(
+            filled, from_left, (index - lap) % count * rows, axis=1
+        )
+        if lap < count - halfway:
+            from_right = lax.ppermute(from_right, "fsdp", backward)
+            filled = lax.dynamic_update_slice_in_dim(
+                filled, from_right, (index + lap) % count * rows, axis=1
+            )
+    gathered = filled
     gram = lax.dot_general(
         gathered, gathered, (((0,), (0,)), ((), ())), preferred_element_type=jnp.float32
     )

time: 155 us -> 128 us (0.83)
  waiting for transfers between devices: 120 us -> 99.1 us
  between operations: 13.4 us -> 0.06 us
  starting transfers between devices: 0.01 us -> 5.1 us
  local copies, waits for them, and re-layouts: 1.57 us -> 5.81 us
  matrix products: 20.1 us -> 17.5 us
    all_gather x1 -> x0, waiting for transfers between devices: 119 us -> none  [on_device_columns(): gathered = lax.all_gather(iterate[0], 'fsdp', axis=1, tiled=True)]
    ppermute x0 -> x3, waiting for transfers between devices: none -> 99.1 us  [the longest x2 68 us: on_device_columns(): from_left = lax.ppermute(from_left, 'fsdp', upward)]
    ppermute x0 -> x3, starting transfers between devices: none -> 5.1 us  [the longest x2 3.03 us: on_device_columns(): from_left = lax.ppermute(from_left, 'fsdp', upward)]
    dot_general x1, matrix products: 12 us -> 8.32 us  [on_device_columns(): lax.dot_general(gathered, gathered, (((0,), (0,)), ((), ())), preferred_e...]
    unnamed x0 -> x4, local copies, waits for them, and re-layouts: none -> 2.65 us
    dynamic_update_slice x0 -> x4, local copies, waits for them, and re-layouts: none -> 2.37 us  [the longest x1 1.65 us: on_device_columns(): lax.dynamic_update_slice_in_dim(filled, from_right, (index + lap) % count...]
  transfers between devices with their start and end apart: 1 -> 3, of which waited for: 1 -> 3; matrix products, arithmetic and copies ran while one was open for 0% -> 2% of each run, Pallas kernels for 0% -> 0%
where the time goes in v1:
time: 128 us
  waiting for transfers between devices  99.1 us (77%)
  matrix products  17.5 us (14%)
  local copies, waits for them, and re-layouts  5.81 us (5%)
  starting transfers between devices  5.1 us (4%)
    ppermute x2, waiting for transfers between devices, on_device_columns(): from_left = lax.ppermute(from_left, 'fsdp', upward)  68 us
    ppermute x1, waiting for transfers between devices, on_device_columns(): from_right = lax.ppermute(from_right, 'fsdp', backward)  31.1 us
    dot_general x1, matrix products, on_device_columns(): jnp.dot(gathered, mixing.astype(jnp.bfloat16), preferred_element_type=jnp...  9.2 us
    dot_general x1, matrix products, on_device_columns(): lax.dot_general(gathered, gathered, (((0,), (0,)), ((), ())), preferred_e...  8.32 us
    ppermute x2, starting transfers between devices, on_device_columns(): from_left = lax.ppermute(from_left, 'fsdp', upward)  3.03 us
    unnamed x4, local copies, waits for them, and re-layouts  2.65 us
  transfers between devices with their start and end apart: 3, of which 3 were waited for; matrix products, arithmetic and copies ran while one was open for 2% of the time, Pallas kernels for 0%

profile of v1, /device:TPU:0, one launch (start us, length us, event | category | flops | bytes accessed | tf_op | source)
XLA Modules:
  0.0 127.6 jit_solution(971018339744226650)
XLA Ops:
  0.0 0.0 copy-start.1
  0.0 3.0 %collective-permute-start = (bf16[3072,256]{1,0:T(8,128)(2,1)}, bf16[3072,256]{1,0:T(8,128)(2,1)S(1)}, u32[]{:S(2)}, u32[]{:S(2)}) collective-permute-start(bf16[3072,256]{1,0:T(8,128)(2,1)} %bitcast.7), channel_id=1, source_target_pairs={{0,4},{4,8},{8,12},{12,0},{1,5},{5,9},{9,13},{13,1},{2,6},{6,10},{... | collective-permute-start | bytes 4718600 | tf_op jit(solution)/shard_map/ppermute | solution.py:76
  3.0 2.1 %collective-permute-start.1 = (bf16[3072,256]{1,0:T(8,128)(2,1)}, bf16[3072,256]{1,0:T(8,128)(2,1)}, u32[]{:S(2)}, u32[]{:S(2)}) collective-permute-start(bf16[3072,256]{1,0:T(8,128)(2,1)} %bitcast.8), channel_id=1, source_target_pairs={{0,12},{4,0},{8,4},{12,8},{1,13},{5,1},{9,5},{13,9},{2,14},{6,2},{... | collective-permute-start | bytes 4718600 | tf_op jit(solution)/shard_map/ppermute | solution.py:81
  5.1 35.5 %collective-permute-done = bf16[3072,256]{1,0:T(8,128)(2,1)S(1)} collective-permute-done((bf16[3072,256]{1,0:T(8,128)(2,1)}, bf16[3072,256]{1,0:T(8,128)(2,1)S(1)}, u32[]{:S(2)}, u32[]{:S(2)}) %collective-permute-start) | collective-permute-done | bytes 1572896 | tf_op jit(solution)/shard_map/ppermute | solution.py:76
  40.6 0.0 collective-permute-start.2
  40.6 0.8 broadcast_in_dim.6
  41.4 0.0 copy-done.1
  41.4 0.2 constant_dynamic-update-slice_fusion.3
  41.7 0.2 constant_dynamic-update-slice_fusion.2
  41.9 31.1 %collective-permute-done.1 = bf16[3072,256]{1,0:T(8,128)(2,1)} collective-permute-done((bf16[3072,256]{1,0:T(8,128)(2,1)}, bf16[3072,256]{1,0:T(8,128)(2,1)}, u32[]{:S(2)}, u32[]{:S(2)}) %collective-permute-start.1) | collective-permute-done | bytes 1572896 | tf_op jit(solution)/shard_map/ppermute | solution.py:81
  73.1 1.6 %constant_dynamic-update-slice_fusion.1 = bf16[3072,1024]{1,0:T(8,128)(2,1)S(1)} fusion(bf16[3072,1024]{1,0:T(8,128)(2,1)S(1)} %constant_dynamic-update-slice_fusion.2, bf16[3072,256]{1,0:T(8,128)(2,1)} %collective-permute-done.1, s32[]{:T(128)S(6)} %select_n.32), kind=kLoop, calls=%fused_computation.12 | loop fusion | bytes 3145732 | tf_op jit(solution)/shard_map/dynamic_update_slice | solution.py:82
  74.7 32.5 %collective-permute-done.2 = bf16[3072,256]{1,0:T(8,128)(2,1)S(1)} collective-permute-done((bf16[3072,256]{1,0:T(8,128)(2,1)S(1)}, bf16[3072,256]{1,0:T(8,128)(2,1)S(1)}, u32[]{:S(2)}, u32[]{:S(2)}) %collective-permute-start.2) | collective-permute-done | bytes 1572896 | tf_op jit(solution)/shard_map/ppermute | solution.py:76
  107.2 0.2 constant_dynamic-update-slice_fusion
  107.4 0.0 copy-start
  107.4 2.6 %copy-done = bf16[3072,1024]{1,0:T(8,128)(2,1)} copy-done((bf16[3072,1024]{1,0:T(8,128)(2,1)}, bf16[3072,1024]{1,0:T(8,128)(2,1)S(1)}, u32[]{:S(2)}) %copy-start) | copy-done | bytes 6291480
  110.1 8.3 %fusion.19 = f32[1024,1024]{1,0:T(8,128)} fusion(bf16[3072,1024]{1,0:T(8,128)(2,1)S(1)} %constant_dynamic-update-slice_fusion), kind=kOutput, calls=%fused_computation.21 | convolution fusion | flops 6442450944 | bytes 10485760 | tf_op jit(solution)/shard_map/dot_general | solution.py:86
  118.4 9.2 %fusion = bf16[1,3072,256]{2,1,0:T(8,128)(2,1)} fusion(bf16[3072,1024]{1,0:T(8,128)(2,1)} %copy-done, f32[1024,1024]{1,0:T(8,128)} %fusion.19, s32[]{:T(128)S(6)} %select_n.28, s32[256]{0:T(256)S(1)} %iota_add_fusion), kind=kOutput, calls=%fused_computation.1 | convolution fusion | flops 2151677952 | bytes 14157824 | tf_op jit(solution)/shard_map/dot_general | solution.py:96
  (1 shorter events, 0.0 us)
Async XLA Ops:
  0.0 41.4 %copy-start.1 = (bf16[1,3072,256]{2,1,0:T(8,128)(2,1)S(1)}, bf16[1,3072,256]{2,1,0:T(8,128)(2,1)}, u32[]{:S(2)}) copy-start(bf16[1,3072,256]{2,1,0:T(8,128)(2,1)} %param.1) | copy-start | bytes 4718596
  0.0 40.6 %collective-permute-start = (bf16[3072,256]{1,0:T(8,128)(2,1)}, bf16[3072,256]{1,0:T(8,128)(2,1)S(1)}, u32[]{:S(2)}, u32[]{:S(2)}) collective-permute-start(bf16[3072,256]{1,0:T(8,128)(2,1)} %bitcast.7), channel_id=1, source_target_pairs={{0,4},{4,8},{8,12},{12,0},{1,5},{5,9},{9,13},{13,1},{2,6},{6,10},{... | collective-permute-start | bytes 4718600 | tf_op jit(solution)/shard_map/ppermute | solution.py:76
  3.0 70.0 %collective-permute-start.1 = (bf16[3072,256]{1,0:T(8,128)(2,1)}, bf16[3072,256]{1,0:T(8,128)(2,1)}, u32[]{:S(2)}, u32[]{:S(2)}) collective-permute-start(bf16[3072,256]{1,0:T(8,128)(2,1)} %bitcast.8), channel_id=1, source_target_pairs={{0,12},{4,0},{8,4},{12,8},{1,13},{5,1},{9,5},{13,9},{2,14},{6,2},{... | collective-permute-start | bytes 4718600 | tf_op jit(solution)/shard_map/ppermute | solution.py:81
  40.6 66.6 %collective-permute-start.2 = (bf16[3072,256]{1,0:T(8,128)(2,1)S(1)}, bf16[3072,256]{1,0:T(8,128)(2,1)S(1)}, u32[]{:S(2)}, u32[]{:S(2)}) collective-permute-start(bf16[3072,256]{1,0:T(8,128)(2,1)S(1)} %collective-permute-done), channel_id=1, source_target_pairs={{0,4},{4,8},{8,12},{12,0},{1,5},{5,9},{9,13},{13,1},{2,6},{6,10},{... | collective-permute-start | bytes 4718600 | tf_op jit(solution)/shard_map/ppermute | solution.py:76
  107.4 2.7 %copy-start = (bf16[3072,1024]{1,0:T(8,128)(2,1)}, bf16[3072,1024]{1,0:T(8,128)(2,1)S(1)}, u32[]{:S(2)}) copy-start(bf16[3072,1024]{1,0:T(8,128)(2,1)S(1)} %constant_dynamic-update-slice_fusion) | copy-start | bytes 18874372
